TPU v7x, 512 devices: a whole 4x4x16 slice. The times are simulated.
512 devices in a mesh: group: 16 (over x, y), dev: 32 (over z, core).
Axes of the slice: x: 4, y: 4, z: 16, core: 2. Of those that a mesh axis runs over, the one named last changes fastest.
Arguments:
- embeddings: bfloat16 [655360, 768], P(('group', 'dev')), may hold values from -6 to 6
- projection: bfloat16 [256, 768], replicated, may hold values from -0.21875 to 0.21875
- triplets: int32 [3, 1048576], P(None, ('group', 'dev')), may hold values from 0 to 3327, as said below
- cotangent: float32 [1048576], P(('group', 'dev')), may hold values from -24 to 24
- wanted_rows: int32 [8192, 128], P(('group', 'dev')), may hold values from -1 to 1279, as said below
Outputs:
- row_grad: bfloat16 [655360, 768], P(('group', 'dev'))
- weight_grad: float32 [256, 768], replicated
Inputs may be any that keep to these rules, and one draw needn't show every extreme that they name: `wanted_rows`: in each list the live entries come first and are distinct rows of the owning device, the rest are -1; each list holds from 128 // 4 (at least 1) to 128 live entries; all lists of some group of requesters are full, and all lists sent to some group are full. `triplets`: anchors are below 1280; a positive or negative below 1280 is one of the device's own rows, else 1280 + h * 128 + s names a live slot s of the device's list for group h.
All inputs are finite; a program needn't handle non-finite values.
Results may differ from a plain program's by a relative error of at most 0.0058.
Values may be sent and summed in bfloat16 or wider, within the bound.
No kernel may reach another device: no remote copies, remote signals or barrier semaphores. Data moves between devices by JAX's collectives and lax.ppermute only.
A program may use at most 64 MiB of HBM per device.

v0:
```python
import math
import jax
import jax.numpy as jnp
from jax import lax
from jax.sharding import PartitionSpec as P

distance_scale = 0.0625
margin = 1.0
pull_share = 0.5


def triplet_gradients(lookup, triple, cotangent):
    anchor_rows = lookup[triple[0]].astype(jnp.float32)
    positive_rows = lookup[triple[1]].astype(jnp.float32)
    negative_rows = lookup[triple[2]].astype(jnp.float32)
    to_positive = anchor_rows - positive_rows
    to_negative = anchor_rows - negative_rows
    near = distance_scale * jnp.sum(to_positive * to_positive, axis=1)
    far = distance_scale * jnp.sum(to_negative * to_negative, axis=1)
    hinge_gate = jax.nn.sigmoid(margin + near - far)
    pull_factor = 2.0 * distance_scale * cotangent * (1.0 - pull_share + pull_share * hinge_gate)
    push_factor = 2.0 * distance_scale * cotangent * pull_share * hinge_gate
    pull_term = pull_factor[:, None] * to_positive
    push_term = push_factor[:, None] * to_negative
    gradient = jnp.zeros(lookup.shape, jnp.float32)
    gradient = gradient.at[triple[0]].add(pull_term - push_term)
    gradient = gradient.at[triple[1]].add(-pull_term)
    gradient = gradient.at[triple[2]].add(push_term)
    return gradient


def local(embeddings, projection, triplets, cotangent, wanted_rows):
    shard_rows = embeddings.shape[0]
    rank_width = projection.shape[0]
    groups = lax.axis_size("group")
    contract = (((1,), (1,)), ((), ()))
    own_projected = lax.dot_general(
        embeddings, projection, contract, preferred_element_type=jnp.float32
    ).astype(jnp.bfloat16)
    wanted = lax.all_to_all(wanted_rows, "group", split_axis=0, concat_axis=0, tiled=True)
    served_index = jnp.maximum(wanted, 0)
    served = own_projected[served_index]
    fetched = lax.all_to_all(served, "group", split_axis=0, concat_axis=0, tiled=True)
    lookup = jnp.concatenate([own_projected, fetched.reshape(-1, rank_width)], axis=0)
    gradient = triplet_gradients(lookup, triplets, cotangent)
    remote_grad = gradient[shard_rows:].reshape(groups, -1, rank_width).astype(jnp.bfloat16)
    returned = lax.all_to_all(remote_grad, "group", split_axis=0, concat_axis=0, tiled=True)
    row_total = (
        gradient[:shard_rows]
        .at[served_index.reshape(-1)]
        .add(returned.reshape(-1, rank_width).astype(jnp.float32))
    )
    row_rounded = row_total.astype(jnp.bfloat16)
    row_grad = jnp.dot(row_rounded, projection, preferred_element_type=jnp.float32).astype(
        jnp.bfloat16
    )
    partial_value = lax.dot_general(
        row_rounded, embeddings, (((0,), (0,)), ((), ())), preferred_element_type=jnp.float32
    )
    factor = 1.0 / math.sqrt(cotangent.shape[0] * groups * lax.axis_size("dev"))
    weight_total = lax.psum(partial_value, ("group", "dev"))
    return (row_grad, weight_total * factor)


def solution(mesh):
    return jax.shard_map(
        local,
        mesh=mesh,
        in_specs=(
            P(("group", "dev"), None),
            P(),
            P(None, ("group", "dev")),
            P(("group", "dev")),
            P(("group", "dev"), None),
        ),
        out_specs=(P(("group", "dev"), None), P()),
        check_vma=False,
    )
```

profile of v0, /device:TPU:2, one launch (start us, length us, event | category | flops | bytes accessed | tf_op | source)
XLA Modules:
  0.0 648.8 jit_solution(12373123322807966387)
XLA Ops:
  7.2 0.0 copy-start
  7.2 9.3 %all-to-all-start = ((s32[16,1,128]{2,1,0:T(1,128)}), s32[16,1,128]{2,1,0:T(1,128)S(1)}, u32[]{:S(2)}, u32[]{:S(2)}) async-start(s32[16,1,128]{2,1,0:T(1,128)} %bitcast.29), calls=%async_computation | async-start | bytes 16384 | tf_op jit(solution)/shard_map/all_to_all | solution.py:40
  16.5 0.0 copy-done
  16.5 1.7 convolution_convert_fusion.1
  18.2 4.5 all-to-all-done
  22.7 9.1 %gather_fusion = bf16[2048,256]{1,0:T(8,128)(2,1)} fusion(bf16[1280,256]{1,0:T(8,128)(2,1)S(1)} %convolution_convert_fusion.1, s32[2048]{0:T(1024)S(1)} %broadcast_clamp_fusion.3), kind=kCustom, calls=%fused_computation | custom fusion | bytes 2105344 | tf_op jit(solution)/shard_map/gather | solution.py:42
  31.8 0.0 copy-start.1
  31.8 5.7 all-to-all-start.1
  37.4 0.0 copy-done.1
  37.5 12.2 %all-to-all-done.1 = bf16[16,128,256]{2,1,0:T(8,128)(2,1)} async-done(((bf16[16,128,256]{2,1,0:T(8,128)(2,1)}), bf16[16,128,256]{2,1,0:T(8,128)(2,1)}, u32[]{:S(2)}, u32[]{:S(2)}) %all-to-all-start.1) | async-done | bytes 1048608 | tf_op jit(solution)/shard_map/all_to_all | solution.py:43
  49.7 2.5 pad_maximum_fusion
  52.2 8.3 %gather_fusion.1 = bf16[2048,256]{1,0:T(8,128)(2,1)S(1)} fusion(bf16[3328,256]{1,0:T(8,128)(2,1)} %pad_maximum_fusion, s32[2048]{0:T(1024)S(1)} %broadcast_clamp_fusion.2), kind=kCustom, calls=%fused_computation.1 | custom fusion | bytes 2105344 | tf_op jit(solution)/shard_map/gather | solution.py:13
  60.5 10.1 %gather_fusion.3 = bf16[2048,256]{1,0:T(8,128)(2,1)} fusion(bf16[3328,256]{1,0:T(8,128)(2,1)} %pad_maximum_fusion, s32[2048]{0:T(1024)S(1)} %broadcast_clamp_fusion), kind=kCustom, calls=%fused_computation.3 | custom fusion | bytes 2105344 | tf_op jit(solution)/shard_map/gather | solution.py:15
  70.7 10.1 %gather_fusion.2 = bf16[2048,256]{1,0:T(8,128)(2,1)} fusion(bf16[3328,256]{1,0:T(8,128)(2,1)} %pad_maximum_fusion, s32[2048]{0:T(1024)S(1)} %broadcast_clamp_fusion.1), kind=kCustom, calls=%fused_computation.2 | custom fusion | bytes 2105344 | tf_op jit(solution)/shard_map/gather | solution.py:14
  80.8 0.0 copy-start.2
  80.8 2.5 multiply_reduce_fusion.1
  83.3 0.0 copy-done.2
  83.3 15.1 %scatter_custom_fusion = f32[3328,256]{1,0:T(8,128)} fusion(s32[2048]{0:T(1024)S(1)} %bitcast.28, bf16[2048,256]{1,0:T(8,128)(2,1)} %gather_fusion.3, bf16[2048,256]{1,0:T(8,128)(2,1)S(1)} %gather_fusion.1, bf16[2048,256]{1,0:T(8,128)(2,1)} %gather_fusion.2, f32[]{:T(128)} %constant.8.clone.1, f32[2048]{0:T(1024)S(1)} %get-tuple-element.8, ...), kind=kCustom, calls=%fused_computation.17 | custom fusion | flops 4718592 | bytes 6569988 | tf_op jit(solution)/shard_map/scatter-add | solution.py:26
  98.4 16.7 %scatter_custom_fusion.1 = f32[3328,256]{1,0:T(8,128)} fusion(f32[3328,256]{1,0:T(8,128)} %scatter_custom_fusion, s32[2048]{0:T(1024)S(1)} %bitcast.26, bf16[2048,256]{1,0:T(8,128)(2,1)} %gather_fusion.2, bf16[2048,256]{1,0:T(8,128)(2,1)S(1)} %gather_fusion.1, f32[2048]{0:T(1024)S(1)} %get-tuple-element.7), kind=kCustom, calls=%fused_computation.15 | custom fusion | flops 3145728 | bytes 5513216 | tf_op jit(solution)/shard_map/scatter-add | solution.py:27
  115.1 16.6 %scatter_custom_fusion.2 = f32[3328,256]{1,0:T(8,128)} fusion(f32[3328,256]{1,0:T(8,128)} %scatter_custom_fusion.1, s32[2048]{0:T(1024)S(1)} %bitcast.24, bf16[2048,256]{1,0:T(8,128)(2,1)} %gather_fusion.3, bf16[2048,256]{1,0:T(8,128)(2,1)S(1)} %gather_fusion.1, f32[2048]{0:T(1024)S(1)} %get-tuple-element.8), kind=kCustom, calls=%fused_computation.23 | custom fusion | flops 2621440 | bytes 5513216 | tf_op jit(solution)/shard_map/scatter-add | solution.py:28
  131.7 2.7 slice.38
  134.4 6.3 all-to-all-start.2
  140.7 0.0 all-reduce.2.cloned.1.call-start
  140.8 1.4 slice.32
  142.2 9.6 %all-to-all-done.2 = bf16[16,128,256]{2,1,0:T(8,128)(2,1)} async-done(((bf16[16,128,256]{2,1,0:T(8,128)(2,1)}), bf16[16,128,256]{2,1,0:T(8,128)(2,1)}, u32[]{:S(2)}, u32[]{:S(2)}) %all-to-all-start.2) | async-done | bytes 1048608 | tf_op jit(solution)/shard_map/all_to_all | solution.py:47
  151.7 13.6 %scatter_custom_fusion.3 = f32[1280,256]{1,0:T(8,128)S(1)} fusion(f32[1280,256]{1,0:T(8,128)S(1)} %slice.32, s32[2048]{0:T(1024)S(1)} %bitcast.22, bf16[2048,256]{1,0:T(8,128)(2,1)} %bitcast.12), kind=kCustom, calls=%fused_computation.13 | custom fusion | flops 1048576 | bytes 2359296 | tf_op jit(solution)/shard_map/scatter-add | solution.py:51
  165.3 1.6 fusion.18
  166.9 0.0 all-reduce.2.cloned.1.call-update
  166.9 2.9 convolution_convert_fusion
  169.9 470.0 %all-reduce.2.cloned.1.call-done = f32[256,768]{1,0:T(8,128)} async-done(((f32[256,768]{1,0:T(8,128)}), f32[256,768]{1,0:T(8,128)}) %all-reduce.2.cloned.1.call-update) | async-done | bytes 786448 | tf_op jit(solution)/shard_map/psum | solution.py:61
  639.9 2.1 broadcast_multiply_fusion
  (7 shorter events, 0.1 us)
Async XLA Ops:
  7.2 9.3 %copy-start = (bf16[1280,768]{1,0:T(8,128)(2,1)S(1)}, bf16[1280,768]{1,0:T(8,128)(2,1)}, u32[]{:S(2)}) copy-start(bf16[1280,768]{1,0:T(8,128)(2,1)} %param.5) | copy-start | bytes 5898244
  7.2 15.5 %all-to-all-start = ((s32[16,1,128]{2,1,0:T(1,128)}), s32[16,1,128]{2,1,0:T(1,128)S(1)}, u32[]{:S(2)}, u32[]{:S(2)}) async-start(s32[16,1,128]{2,1,0:T(1,128)} %bitcast.29), calls=%async_computation | async-start | bytes 16384 | tf_op jit(solution)/shard_map/all_to_all | solution.py:40
  31.8 5.7 copy-start.1
  31.8 17.9 %all-to-all-start.1 = ((bf16[16,128,256]{2,1,0:T(8,128)(2,1)}), bf16[16,128,256]{2,1,0:T(8,128)(2,1)}, u32[]{:S(2)}, u32[]{:S(2)}) async-start(bf16[16,128,256]{2,1,0:T(8,128)(2,1)} %bitcast.20), calls=%async_computation.1 | async-start | bytes 2097152 | tf_op jit(solution)/shard_map/all_to_all | solution.py:43
  80.8 2.5 copy-start.2
  134.4 17.3 %all-to-all-start.2 = ((bf16[16,128,256]{2,1,0:T(8,128)(2,1)}), bf16[16,128,256]{2,1,0:T(8,128)(2,1)}, u32[]{:S(2)}, u32[]{:S(2)}) async-start(bf16[16,128,256]{2,1,0:T(8,128)(2,1)} %bitcast.10), calls=%async_computation.2 | async-start | bytes 2097152 | tf_op jit(solution)/shard_map/all_to_all | solution.py:47
  140.7 499.1 %all-reduce.2.cloned.1.call-start = ((), (), s32[]{:S(2)}) async-start(), calls=%async_computation.3 | async-start | bytes 1572864 | tf_op jit(solution)/shard_map/psum | solution.py:61
Sparse Core Ops, SparseCore 0:
  167.0 472.7 all-reduce.1
where the time goes:
time: 650 us; the launch traced here: 649 us
  waiting for transfers between devices  496 us (76%)
  other arithmetic  69.2 us (11%)
  local copies, waits for them, and re-layouts  41.7 us (6%)
  starting transfers between devices  21.3 us (3%)
  between operations  14.1 us (2%)
    psum x1, waiting for transfers between devices, local(): weight_total = lax.psum(partial_value, ('group', 'dev'))  470 us
    scatter-add x1, other arithmetic, triplet_gradients(): gradient = gradient.at[triple[1]].add(-pull_term)  16.7 us
    scatter-add x1, other arithmetic, triplet_gradients(): gradient = gradient.at[triple[2]].add(push_term)  16.6 us
    scatter-add x1, other arithmetic, triplet_gradients(): gradient = gradient.at[triple[0]].add(pull_term - push_term)  15.1 us
    scatter-add x1, other arithmetic, local(): row_total = gradient[:shard_rows].at[served_index.reshape(-1)].add(return...  13.6 us
  transfers between devices with their start and end apart: 4, of which 4 were waited for; matrix products, arithmetic and copies ran while one was open for 1% of the time, Pallas kernels for 0%

commit v1 on v0

--- a/solution.py
+++ b/solution.py
@@ -1,3 +1,4 @@
+import functools
 import math
 import jax
 import jax.numpy as jnp
@@ -7,6 +8,13 @@
 distance_scale = 0.0625
 margin = 1.0
 pull_share = 0.5
+
+
+def _process_flows(page, mesh_dim, axis_key):
+    return jax.lax.psum(jax.lax.psum(page, mesh_dim), axis_key)
+
+
+unite_kinds_over_axis = functools.partial(_process_flows, mesh_dim="dev", axis_key="group")
 
 
 def triplet_gradients(lookup, triple, cotangent):
@@ -58,7 +66,7 @@
         row_rounded, embeddings, (((0,), (0,)), ((), ())), preferred_element_type=jnp.float32
     )
     factor = 1.0 / math.sqrt(cotangent.shape[0] * groups * lax.axis_size("dev"))
-    weight_total = lax.psum(partial_value, ("group", "dev"))
+    weight_total = unite_kinds_over_axis(partial_value)
     return (row_grad, weight_total * factor)
 
 

time: 650 us -> 511 us (0.79)
  the two profiles are of different devices: /device:TPU:2 before, /device:TPU:32 now
where the time goes in v1:
time: 511 us; the launch traced here: 510 us
  waiting for transfers between devices  363 us (71%)
  other arithmetic  69.1 us (14%)
  local copies, waits for them, and re-layouts  41.7 us (8%)
  starting transfers between devices  16.1 us (3%)
  between operations  14.2 us (3%)
  matrix products  6.25 us (1%)
    psum x2, waiting for transfers between devices, _process_flows(): return jax.lax.psum(jax.lax.psum(page, mesh_dim), axis_key)  328 us
    scatter-add x1, other arithmetic, triplet_gradients(): gradient = gradient.at[triple[1]].add(-pull_term)  16.7 us
    scatter-add x1, other arithmetic, triplet_gradients(): gradient = gradient.at[triple[2]].add(push_term)  16.6 us
    all_to_all x1, waiting for transfers between devices, local(): lax.all_to_all(served, 'group', split_axis=0, concat_axis=0, tiled=True)  15.9 us
    scatter-add x1, other arithmetic, triplet_gradients(): gradient = gradient.at[triple[0]].add(pull_term - push_term)  15.1 us
    all_to_all x1, waiting for transfers between devices, local(): lax.all_to_all(remote_grad, 'group', split_axis=0, concat_axis=0, tiled=T...  13.7 us
    scatter-add x1, other arithmetic, local(): row_total = gradient[:shard_rows].at[served_index.reshape(-1)].add(return...  13.5 us
  transfers between devices with their start and end apart: 5, of which 5 were waited for; matrix products, arithmetic and copies ran while one was open for 1% of the time, Pallas kernels for 0%

profile of v1, /device:TPU:32, one launch (start us, length us, event | category | flops | bytes accessed | tf_op | source)
XLA Modules:
  0.0 510.2 jit_solution(15778988758152788602)
XLA Ops:
  7.2 0.0 copy-start
  7.2 7.2 %all-to-all-start = ((s32[16,1,128]{2,1,0:T(1,128)}), s32[16,1,128]{2,1,0:T(1,128)S(1)}, u32[]{:S(2)}, u32[]{:S(2)}) async-start(s32[16,1,128]{2,1,0:T(1,128)} %bitcast.29), calls=%async_computation | async-start | bytes 16384 | tf_op jit(solution)/shard_map/all_to_all | solution.py:48
  14.4 0.0 copy-done
  14.4 1.7 convolution_convert_fusion.1
  16.1 5.8 %all-to-all-done = s32[16,1,128]{2,1,0:T(1,128)S(1)} async-done(((s32[16,1,128]{2,1,0:T(1,128)}), s32[16,1,128]{2,1,0:T(1,128)S(1)}, u32[]{:S(2)}, u32[]{:S(2)}) %all-to-all-start) | async-done | bytes 8224 | tf_op jit(solution)/shard_map/all_to_all | solution.py:48
  21.9 9.1 %gather_fusion = bf16[2048,256]{1,0:T(8,128)(2,1)} fusion(bf16[1280,256]{1,0:T(8,128)(2,1)S(1)} %convolution_convert_fusion.1, s32[2048]{0:T(1024)S(1)} %broadcast_clamp_fusion.3), kind=kCustom, calls=%fused_computation | custom fusion | bytes 2105344 | tf_op jit(solution)/shard_map/gather | solution.py:50
  30.9 0.0 copy-start.1
  30.9 4.5 all-to-all-start.1
  35.4 0.0 copy-done.1
  35.5 15.9 %all-to-all-done.1 = bf16[16,128,256]{2,1,0:T(8,128)(2,1)} async-done(((bf16[16,128,256]{2,1,0:T(8,128)(2,1)}), bf16[16,128,256]{2,1,0:T(8,128)(2,1)}, u32[]{:S(2)}, u32[]{:S(2)}) %all-to-all-start.1) | async-done | bytes 1048608 | tf_op jit(solution)/shard_map/all_to_all | solution.py:51
  51.4 2.5 pad_maximum_fusion
  53.9 8.3 %gather_fusion.1 = bf16[2048,256]{1,0:T(8,128)(2,1)S(1)} fusion(bf16[3328,256]{1,0:T(8,128)(2,1)} %pad_maximum_fusion, s32[2048]{0:T(1024)S(1)} %broadcast_clamp_fusion.2), kind=kCustom, calls=%fused_computation.1 | custom fusion | bytes 2105344 | tf_op jit(solution)/shard_map/gather | solution.py:21
  62.2 10.1 %gather_fusion.3 = bf16[2048,256]{1,0:T(8,128)(2,1)} fusion(bf16[3328,256]{1,0:T(8,128)(2,1)} %pad_maximum_fusion, s32[2048]{0:T(1024)S(1)} %broadcast_clamp_fusion), kind=kCustom, calls=%fused_computation.3 | custom fusion | bytes 2105344 | tf_op jit(solution)/shard_map/gather | solution.py:23
  72.4 10.1 %gather_fusion.2 = bf16[2048,256]{1,0:T(8,128)(2,1)} fusion(bf16[3328,256]{1,0:T(8,128)(2,1)} %pad_maximum_fusion, s32[2048]{0:T(1024)S(1)} %broadcast_clamp_fusion.1), kind=kCustom, calls=%fused_computation.2 | custom fusion | bytes 2105344 | tf_op jit(solution)/shard_map/gather | solution.py:22
  82.4 0.0 copy-start.2
  82.5 2.5 multiply_reduce_fusion.1
  85.0 0.0 copy-done.2
  85.0 15.1 %scatter_custom_fusion = f32[3328,256]{1,0:T(8,128)} fusion(s32[2048]{0:T(1024)S(1)} %bitcast.28, bf16[2048,256]{1,0:T(8,128)(2,1)} %gather_fusion.3, bf16[2048,256]{1,0:T(8,128)(2,1)S(1)} %gather_fusion.1, bf16[2048,256]{1,0:T(8,128)(2,1)} %gather_fusion.2, f32[]{:T(128)} %constant.8.clone.1, f32[2048]{0:T(1024)S(1)} %get-tuple-element.8, ...), kind=kCustom, calls=%fused_computation.17 | custom fusion | flops 4718592 | bytes 6569988 | tf_op jit(solution)/shard_map/scatter-add | solution.py:34
  100.1 16.7 %scatter_custom_fusion.1 = f32[3328,256]{1,0:T(8,128)} fusion(f32[3328,256]{1,0:T(8,128)} %scatter_custom_fusion, s32[2048]{0:T(1024)S(1)} %bitcast.26, bf16[2048,256]{1,0:T(8,128)(2,1)} %gather_fusion.2, bf16[2048,256]{1,0:T(8,128)(2,1)S(1)} %gather_fusion.1, f32[2048]{0:T(1024)S(1)} %get-tuple-element.7), kind=kCustom, calls=%fused_computation.15 | custom fusion | flops 3145728 | bytes 5513216 | tf_op jit(solution)/shard_map/scatter-add | solution.py:35
  116.8 16.6 %scatter_custom_fusion.2 = f32[3328,256]{1,0:T(8,128)} fusion(f32[3328,256]{1,0:T(8,128)} %scatter_custom_fusion.1, s32[2048]{0:T(1024)S(1)} %bitcast.24, bf16[2048,256]{1,0:T(8,128)(2,1)} %gather_fusion.3, bf16[2048,256]{1,0:T(8,128)(2,1)S(1)} %gather_fusion.1, f32[2048]{0:T(1024)S(1)} %get-tuple-element.8), kind=kCustom, calls=%fused_computation.23 | custom fusion | flops 2621440 | bytes 5513216 | tf_op jit(solution)/shard_map/scatter-add | solution.py:36
  133.4 2.7 slice.38
  136.1 4.3 all-to-all-start.2
  140.4 0.0 all-reduce.3.cloned.1.call-start
  140.5 1.4 slice.32
  141.9 13.7 %all-to-all-done.2 = bf16[16,128,256]{2,1,0:T(8,128)(2,1)} async-done(((bf16[16,128,256]{2,1,0:T(8,128)(2,1)}), bf16[16,128,256]{2,1,0:T(8,128)(2,1)}, u32[]{:S(2)}, u32[]{:S(2)}) %all-to-all-start.2) | async-done | bytes 1048608 | tf_op jit(solution)/shard_map/all_to_all | solution.py:55
  155.6 13.5 %scatter_custom_fusion.3 = f32[1280,256]{1,0:T(8,128)S(1)} fusion(f32[1280,256]{1,0:T(8,128)S(1)} %slice.32, s32[2048]{0:T(1024)S(1)} %bitcast.22, bf16[2048,256]{1,0:T(8,128)(2,1)} %bitcast.12), kind=kCustom, calls=%fused_computation.13 | custom fusion | flops 1048576 | bytes 2359296 | tf_op jit(solution)/shard_map/scatter-add | solution.py:59
  169.1 1.6 fusion.18
  170.7 0.0 all-reduce.3.cloned.1.call-update
  170.7 0.0 all-reduce.5.cloned.1.call-start
  170.8 208.0 %all-reduce.3.cloned.1.call-done = f32[256,768]{1,0:T(8,128)} async-done(((f32[256,768]{1,0:T(8,128)}), f32[256,768]{1,0:T(8,128)}) %all-reduce.3.cloned.1.call-update) | async-done | bytes 786448 | tf_op jit(solution)/shard_map/psum | solution.py:14
  378.8 0.0 all-reduce.5.cloned.1.call-update
  378.8 3.0 convolution_convert_fusion
  381.7 119.6 %all-reduce.5.cloned.1.call-done = f32[256,768]{1,0:T(8,128)} async-done(((f32[256,768]{1,0:T(8,128)}), f32[256,768]{1,0:T(8,128)}) %all-reduce.5.cloned.1.call-update) | async-done | bytes 786448 | tf_op jit(solution)/shard_map/psum | solution.py:14
  501.3 2.1 broadcast_multiply_fusion
  (7 shorter events, 0.1 us)
Async XLA Ops:
  7.2 7.2 %copy-start = (bf16[1280,768]{1,0:T(8,128)(2,1)S(1)}, bf16[1280,768]{1,0:T(8,128)(2,1)}, u32[]{:S(2)}) copy-start(bf16[1280,768]{1,0:T(8,128)(2,1)} %param.5) | copy-start | bytes 5898244
  7.2 14.7 %all-to-all-start = ((s32[16,1,128]{2,1,0:T(1,128)}), s32[16,1,128]{2,1,0:T(1,128)S(1)}, u32[]{:S(2)}, u32[]{:S(2)}) async-start(s32[16,1,128]{2,1,0:T(1,128)} %bitcast.29), calls=%async_computation | async-start | bytes 16384 | tf_op jit(solution)/shard_map/all_to_all | solution.py:48
  30.9 4.5 copy-start.1
  30.9 20.4 %all-to-all-start.1 = ((bf16[16,128,256]{2,1,0:T(8,128)(2,1)}), bf16[16,128,256]{2,1,0:T(8,128)(2,1)}, u32[]{:S(2)}, u32[]{:S(2)}) async-start(bf16[16,128,256]{2,1,0:T(8,128)(2,1)} %bitcast.20), calls=%async_computation.1 | async-start | bytes 2097152 | tf_op jit(solution)/shard_map/all_to_all | solution.py:51
  82.4 2.5 copy-start.2
  136.1 19.5 %all-to-all-start.2 = ((bf16[16,128,256]{2,1,0:T(8,128)(2,1)}), bf16[16,128,256]{2,1,0:T(8,128)(2,1)}, u32[]{:S(2)}, u32[]{:S(2)}) async-start(bf16[16,128,256]{2,1,0:T(8,128)(2,1)} %bitcast.10), calls=%async_computation.2 | async-start | bytes 2097152 | tf_op jit(solution)/shard_map/all_to_all | solution.py:55
  140.4 238.3 %all-reduce.3.cloned.1.call-start = ((), (), s32[]{:S(2)}) async-start(), calls=%async_computation.3 | async-start | bytes 1572864 | tf_op jit(solution)/shard_map/psum | solution.py:14
  170.7 330.6 %all-reduce.5.cloned.1.call-start = ((), (), s32[]{:S(2)}) async-start(), calls=%async_computation.4 | async-start | bytes 1572864 | tf_op jit(solution)/shard_map/psum | solution.py:14
Sparse Core Ops, SparseCore 0:
  170.8 207.8 all-reduce.2
  382.3 118.9 all-reduce.4
